TPU v7x, 256 devices: a whole 4x4x8 slice. The times are simulated.
256 devices in a mesh: dp: 32 (over x, y, core), ctx: 8 (over z).
Axes of the slice: x: 4, y: 4, z: 8, core: 2. Of those that a mesh axis runs over, the one named last changes fastest.
Arguments:
- cotangent: bfloat16 [32, 4096, 8192], P('dp', 'ctx'), may hold values from -6 to 6
- out_weight: bfloat16 [256, 8192], P(None, 'ctx'), may hold values from -0.0625 to 0.0625
- head_input: bfloat16 [32, 4096, 256], P('dp', 'ctx'), may hold values from -6 to 6
- injector: bfloat16 [32, 4096, 128], P('dp', 'ctx'), may hold values from -0.59765625 to 0.59765625
- readout: bfloat16 [32, 4096, 128], P('dp', 'ctx'), may hold values from -0.59765625 to 0.59765625
- decay_code: int32 [32, 4096, 2], P('dp', 'ctx'), may hold values from 1 to 40960
- decay_rate: float32 [2], replicated, may hold values from 4.8828125e-06 to 0.0061035156
- start_state: float32 [32, 8, 2, 128, 128], P('dp', 'ctx'), may hold values from -6 to 6
Outputs:
- gradient_input: bfloat16 [32, 4096, 256], P('dp', 'ctx')
- gradient_injector: float32 [32, 4096, 128], P('dp', 'ctx')
- gradient_readout: float32 [32, 4096, 128], P('dp', 'ctx')
- gradient_weight: float32 [256, 8192], P('ctx', 'dp')
- gradient_rate: float32 [2], replicated
All inputs are finite; a program needn't handle non-finite values.
Results may differ from a plain program's by a relative error of at most 0.0049.
Values may be sent and summed in bfloat16 or wider, within the bound.
No kernel may reach another device: no remote copies, remote signals or barrier semaphores. Data moves between devices by JAX's collectives and lax.ppermute only.
A program may use at most 128 MiB of HBM per device.

v0:
```python
import jax
import jax.numpy as jnp
from jax import lax
from jax.sharding import PartitionSpec as P

precise = lax.Precision.HIGHEST


def carried_in(value, axis, join, neutral):
    count, mine = (lax.axis_size(axis), lax.axis_index(axis))
    pieces = jax.tree.map(lambda part: lax.all_gather(part, axis), value)
    pieces = jax.tree.map(lambda part: part[::-1], pieces)
    mine = count - 1 - mine
    total = jax.tree.map(
        lambda part, zero: jnp.full_like(part, 0) + jnp.asarray(zero, part.dtype), value, neutral
    )

    def lap(position, total):
        longer = join(total, jax.tree.map(lambda part: part[position], pieces))
        return jax.tree.map(lambda new, old: jnp.where(position < mine, new, old), longer, total)

    return lax.fori_loop(0, count - 1, lap, total)


def decay_table(log_decay):
    cumulative = jnp.cumsum(log_decay, axis=0)
    length = log_decay.shape[0]
    row_index = lax.broadcasted_iota(jnp.int32, (length, length), 0)
    col_index = lax.broadcasted_iota(jnp.int32, (length, length), 1)
    causal = (row_index >= col_index)[None]
    spread = cumulative.T[:, :, None] - cumulative.T[:, None, :]
    weights = jnp.where(causal, jnp.exp(jnp.where(causal, spread, 0.0)), 0.0)
    return (cumulative, weights)


def forward_shard(head_input, injector, readout, log_decay, start_state):
    length, heads_count = log_decay.shape
    cumulative, weights = decay_table(log_decay)
    intersection = jnp.dot(readout, injector.T, preferred_element_type=jnp.float32)
    mixing = intersection[None] * weights
    inputs_heads = head_input.reshape(length, heads_count, -1).astype(jnp.float32)
    within = jnp.einsum("hts,shp->thp", mixing, inputs_heads, precision=precise)
    carried = jnp.einsum("tn,hpn->thp", readout.astype(jnp.float32), start_state, precision=precise)
    outputs = within + jnp.exp(cumulative)[:, :, None] * carried
    return outputs.reshape(length, -1).astype(jnp.bfloat16)


def chain_piece(readout, output_grad, log_decay):
    length, heads_count = log_decay.shape
    cumulative = jnp.cumsum(log_decay, axis=0)
    grad_heads = output_grad.reshape(length, heads_count, -1).astype(jnp.float32)
    scaled = jnp.exp(cumulative)[:, :, None] * readout.astype(jnp.float32)[:, None, :]
    adjoint = jnp.einsum("thp,thn->hpn", grad_heads, scaled, precision=precise)
    return (jnp.exp(cumulative[-1]), adjoint)


def backward_shard(head_input, injector, readout, output_grad, log_decay, start_state, incoming):
    length, heads_count = log_decay.shape
    cumulative, weights = decay_table(log_decay)
    inputs_narrow = head_input.reshape(length, heads_count, -1)
    grad_narrow = output_grad.reshape(length, heads_count, -1)
    inputs_heads = inputs_narrow.astype(jnp.float32)
    grad_heads = grad_narrow.astype(jnp.float32)
    inject_float = injector.astype(jnp.float32)
    read_float = readout.astype(jnp.float32)
    intersection = jnp.dot(readout, injector.T, preferred_element_type=jnp.float32)
    mixing = intersection[None] * weights
    to_end = jnp.exp(cumulative[-1][None, :] - cumulative)
    from_start = jnp.exp(cumulative)
    entering = jnp.einsum("sn,hpn->shp", inject_float, incoming, precision=precise)
    grad_input = (
        jnp.einsum("hts,thp->shp", mixing, grad_heads, precision=precise)
        + to_end[:, :, None] * entering
    )
    pairing = (
        jnp.einsum("thp,shp->hts", grad_narrow, inputs_narrow, preferred_element_type=jnp.float32)
        * weights
    )
    through_start = jnp.einsum("thp,hpn->thn", grad_heads, start_state, precision=precise)
    grad_read = jnp.einsum("hts,sn->tn", pairing, inject_float, precision=precise)
    grad_read = grad_read + jnp.einsum("th,thn->tn", from_start, through_start, precision=precise)
    input_state = jnp.einsum("shp,hpn->shn", inputs_heads, incoming, precision=precise)
    grad_inject = jnp.einsum("hts,tn->sn", pairing, read_float, precision=precise)
    grad_inject = grad_inject + jnp.einsum("sh,shn->sn", to_end, input_state, precision=precise)
    products = intersection[None] * pairing
    carried = (
        jnp.einsum("tn,hpn->thp", read_float, start_state, precision=precise)
        * from_start[:, :, None]
    )
    reaching = to_end * jnp.einsum("shn,sn->sh", input_state, inject_float, precision=precise)
    end_term = from_start[-1] * jnp.einsum(
        "hpn,hpn->h", incoming, start_state, precision=precise
    ) + jnp.sum(reaching, axis=0)
    cumul_grad = jnp.sum(products, axis=2).T - jnp.sum(products, axis=1).T
    cumul_grad = cumul_grad + jnp.sum(grad_heads * carried, axis=2) - reaching
    is_last = lax.broadcasted_iota(jnp.int32, (length, 1), 0) == length - 1
    cumul_grad = cumul_grad + jnp.where(is_last, end_term[None, :], 0.0)
    decay_grad = jnp.flip(jnp.cumsum(jnp.flip(cumul_grad, 0), axis=0), 0)
    rate_terms = jnp.sum(decay_grad * log_decay, axis=0)
    return (grad_input.reshape(length, -1).astype(jnp.bfloat16), grad_inject, grad_read, rate_terms)


def combine(earlier, later):
    return (later[0] * earlier[0], later[1] + later[0][:, None, None] * earlier[1])


def local(
    cotangent, out_weight, head_input, injector, readout, decay_code, decay_rate, start_state
):
    grad_out = cotangent[0]
    inputs_local = head_input[0]
    inject_local = injector[0]
    read_local = readout[0]
    state_local = start_state[0, 0]
    length = grad_out.shape[0]
    output_grad = lax.dot_general(
        grad_out,
        lax.all_gather(out_weight, "ctx", axis=1, tiled=True),
        (((1,), (1,)), ((), ())),
        preferred_element_type=jnp.float32,
    ).astype(jnp.bfloat16)
    log_decay = -decay_rate[None, :] * decay_code[0].astype(jnp.float32)
    decay_total, adjoint = chain_piece(read_local, output_grad, log_decay)
    identity = (jnp.ones_like(decay_total), jnp.zeros_like(adjoint))
    incoming = carried_in((decay_total, adjoint), "ctx", combine, identity)[1]
    outputs = forward_shard(inputs_local, inject_local, read_local, log_decay, state_local)
    local_weight = lax.dot_general(
        outputs, grad_out, (((0,), (0,)), ((), ())), preferred_element_type=jnp.float32
    )
    data_part = lax.psum_scatter(local_weight, "dp", scatter_dimension=1, tiled=True)
    weight_part = lax.psum_scatter(data_part, "ctx", scatter_dimension=0, tiled=True)
    grad_input, grad_inject, grad_read, rate_terms = backward_shard(
        inputs_local, inject_local, read_local, output_grad, log_decay, state_local, incoming
    )
    tokens_all = length * lax.axis_size("dp") * lax.axis_size("ctx")
    rate_sum = lax.psum(rate_terms, ("dp", "ctx"))
    return (
        grad_input[None],
        grad_inject[None],
        grad_read[None],
        weight_part,
        rate_sum / tokens_all,
    )


def solution(mesh):
    in_specs = (
        P("dp", "ctx", None),
        P(None, "ctx"),
        P("dp", "ctx", None),
        P("dp", "ctx", None),
        P("dp", "ctx", None),
        P("dp", "ctx", None),
        P(),
        P("dp", "ctx", None, None, None),
    )
    out_specs = (
        P("dp", "ctx", None),
        P("dp", "ctx", None),
        P("dp", "ctx", None),
        P("ctx", "dp"),
        P(),
    )
    return jax.shard_map(local, mesh=mesh, in_specs=in_specs, out_specs=out_specs, check_vma=False)
```

profile of v0, /device:TPU:2, one launch (start us, length us, event | category | flops | bytes accessed | tf_op | source)
XLA Modules:
  0.0 262.4 jit_solution(3269358175071123547)
XLA Ops:
  7.2 0.7 all-gather.5.cloned.1.call-update
  7.9 0.7 neg.4
  8.6 0.8 fusion.61
  9.4 0.6 reduce-window.14
  10.3 0.9 bitcast_convert_fusion.1
  11.5 56.1 %all-gather.5.cloned.1.call-done = bf16[256,8192]{1,0:T(8,128)(2,1)} async-done(((bf16[256,1024]{1,0:T(8,128)(2,1)}), bf16[256,8192]{1,0:T(8,128)(2,1)}) %all-gather.5.cloned.1.call-update) | async-done | bytes 4194320 | tf_op jit(solution)/shard_map/all_gather | solution.py:118
  67.6 6.9 %fusion.26 = bf16[512,256]{0,1:T(8,128)(2,1)S(1)} fusion(bf16[256,8192]{1,0:T(8,128)(2,1)} %all-gather.5.cloned.1.call-done, bf16[1,512,8192]{2,1,0:T(8,128)(2,1)} %param.10), kind=kOutput, calls=%fused_computation.24 | convolution fusion | flops 2147614720 | bytes 12845056 | tf_op jit(solution)/shard_map/dot_general | solution.py:116
  74.6 1.1 fusion.43
  76.8 2.0 fusion.22
  78.7 9.1 %fusion.1 = f32[256,8192]{1,0:T(8,128)} fusion(bf16[512,256]{0,1:T(8,128)(2,1)S(1)} %bitcast.164, bf16[1,512,8192]{2,1,0:T(8,128)(2,1)} %param.10), kind=kOutput, calls=%fused_computation.3 | convolution fusion | flops 2147483648 | bytes 17039360 | tf_op jit(solution)/shard_map/dot_general | solution.py:127
  88.0 14.7 %all-gather.1 = f32[8,1,2]{2,1,0:T(1,128)S(1)} all-gather(f32[1,1,2]{2,1,0:T(1,128)S(1)} %bitcast.175), channel_id=1, replica_groups=mesh['dp'=32,'ctx'=8] {'ctx'}, dimensions={0}, use_global_device_ids=true | all-gather | bytes 72 | tf_op jit(solution)/shard_map/all_gather | solution.py:11
  104.0 4.4 %fusion.45 = f32[512,1,128]{2,1,0:T(1,128)} fusion(f32[512,2,1]{1,2,0:T(1,128)S(1)} %copy.72, f32[512,2,128]{2,0,1:T(8,128)S(1)} %convolution_bitcast_fusion), kind=kOutput, calls=%fused_computation.47 | convolution fusion | flops 1572864 | bytes 790528 | tf_op jit(solution)/shard_map/th,thn->tn/dot_general | solution.py:81
  108.4 2.4 fusion.11
  110.8 2.2 multiply_reduce_fusion
  113.1 1.3 rev.13
  114.5 0.9 while.14
  116.6 0.6 reduce-window.16
  118.2 1.3 fusion.29
  119.5 75.2 %psum.7 = f32[2]{0:T(128)S(1)} all-reduce(f32[2]{0:T(128)S(1)} %multiply_reduce_fusion.3), channel_id=1, replica_groups=mesh['dp'=32,'ctx'=8] {'dp','ctx'}, use_global_device_ids=true, to_apply=%region_14.15 | all-reduce | flops 2 | bytes 16 | tf_op jit(solution)/shard_map/psum | solution.py:136
  194.9 21.4 %reduce-scatter.3.cloned.1.call-done = f32[256,256]{1,0:T(8,128)} async-done(((f32[256,8192]{1,0:T(8,128)}), f32[256,256]{1,0:T(8,128)}) %reduce-scatter.3.cloned.1.call-update) | async-done | bytes 262160 | tf_op jit(solution)/shard_map/reduce_scatter | solution.py:130
  216.7 0.8 copy.62
  217.6 1.7 fusion.30
  219.3 0.5 broadcast_multiply_fusion
  219.8 36.1 %reduce-scatter.5.cloned.1.call-done = f32[32,256]{1,0:T(8,128)} async-done(((f32[256,256]{1,0:T(8,128)}), f32[32,256]{1,0:T(8,128)}) %reduce-scatter.5.cloned.1.call-update) | async-done | bytes 32784 | tf_op jit(solution)/shard_map/reduce_scatter | solution.py:131
  (76 shorter events, 6.6 us)
Async XLA Ops:
  7.2 60.4 %all-gather.5.cloned.1.call-start = ((), (), s32[]{:S(2)}) async-start(), calls=%async_computation.2 | async-start | bytes 4718592 | tf_op jit(solution)/shard_map/all_gather | solution.py:118
  7.9 105.2 %all-gather.7.cloned.1.call-start = ((), (), s32[]{:S(2)}) async-start(), calls=%async_computation.5 | async-start | bytes 1179648 | tf_op jit(solution)/shard_map/all_gather | solution.py:11
  11.5 64.2 %copy-start.4 = (bf16[1,512,256]{2,1,0:T(8,128)(2,1)S(1)}, bf16[1,512,256]{2,1,0:T(8,128)(2,1)}, u32[]{:S(2)}) copy-start(bf16[1,512,256]{2,1,0:T(8,128)(2,1)} %param.12) | copy-start | bytes 786436
  11.5 64.5 %copy-start = (bf16[1,512,128]{2,1,0:T(8,128)(2,1)S(1)}, bf16[1,512,128]{2,1,0:T(8,128)(2,1)}, u32[]{:S(2)}) copy-start(bf16[1,512,128]{2,1,0:T(8,128)(2,1)} %param.13) | copy-start | bytes 393220
  11.5 64.5 %copy-start.1 = (bf16[1,512,128]{2,1,0:T(8,128)(2,1)S(1)}, bf16[1,512,128]{2,1,0:T(8,128)(2,1)}, u32[]{:S(2)}) copy-start(bf16[1,512,128]{2,1,0:T(8,128)(2,1)} %param.14) | copy-start | bytes 393220
  74.5 1.8 copy-start.2
  75.7 140.6 %reduce-scatter.3.cloned.1.call-start = ((), (), s32[]{:S(2)}) async-start(), calls=%async_computation.3 | async-start | bytes 8650752 | tf_op jit(solution)/shard_map/reduce_scatter | solution.py:130
  76.0 32.4 %copy-start.5 = (pred[512,512]{1,0:T(8,128)(4,1)}, pred[512,512]{1,0:T(8,128)(4,1)S(1)}, u32[]{:S(2)}) copy-start(pred[512,512]{1,0:T(8,128)(4,1)S(1)} %iota_compare_fusion) | copy-start | bytes 786436
  87.8 168.0 %reduce-scatter.5.cloned.1.call-start = ((), (), s32[]{:S(2)}) async-start(), calls=%async_computation.4 | async-start | bytes 294912 | tf_op jit(solution)/shard_map/reduce_scatter | solution.py:131
  114.4 3.5 %copy-start.7 = (s32[1,512,2]{1,2,0:T(2,128)S(1)}, s32[1,512,2]{1,2,0:T(2,128)}, u32[]{:S(2)}) copy-start(s32[1,512,2]{1,2,0:T(2,128)} %param.15) | copy-start | bytes 12292
  114.5 3.7 %copy-start.6 = (f32[512,1,128]{2,1,0:T(1,128)S(1)}, f32[512,1,128]{2,1,0:T(1,128)}, u32[]{:S(2)}) copy-start(f32[512,1,128]{2,1,0:T(1,128)} %fusion.45) | copy-start | bytes 786436
  115.5 100.8 %copy-start.3 = (f32[512,2,128]{0,2,1:T(8,128)S(1)}, f32[512,2,128]{0,2,1:T(8,128)}, u32[]{:S(2)}) copy-start(f32[512,2,128]{0,2,1:T(8,128)} %fusion.11) | copy-start | bytes 1572868
Sparse Core Ops, SparseCore 0:
  9.8 57.7 all-gather.4
  75.8 37.3 all-gather.6
  117.2 99.0 reduce-scatter.2
  219.4 36.4 reduce-scatter.4
where the time goes:
time: 263 us; the launch traced here: 262 us
  waiting for transfers between devices  114 us (43%)
  blocking collectives  89.9 us (34%)
  matrix products  33.1 us (13%)
  between operations  14 us (5%)
  other arithmetic  5.93 us (2%)
  local copies, waits for them, and re-layouts  4.61 us (2%)
    psum x1, blocking collectives, local(): rate_sum = lax.psum(rate_terms, ('dp', 'ctx'))  75.2 us
    all_gather x1, waiting for transfers between devices, local(): lax.all_gather(out_weight, 'ctx', axis=1, tiled=True)  56.1 us
    reduce_scatter x1, waiting for transfers between devices, local(): lax.psum_scatter(data_part, 'ctx', scatter_dimension=0, tiled=True)  36.1 us
    reduce_scatter x1, waiting for transfers between devices, local(): lax.psum_scatter(local_weight, 'dp', scatter_dimension=1, tiled=True)  21.4 us
    all_gather x1, blocking collectives, carried_in(): pieces = jax.tree.map(lambda part: lax.all_gather(part, axis), value)  14.7 us
    dot_general x1, matrix products, local(): lax.dot_general(outputs, grad_out, (((0,), (0,)), ((), ())), preferred_el...  9.06 us
    dot_general x1, matrix products, local(): lax.dot_general(grad_out, lax.all_gather(out_weight, 'ctx', axis=1, tiled...  6.93 us
  transfers between devices with their start and end apart: 4, of which 4 were waited for; matrix products, arithmetic and copies ran while one was open for 14% of the time, Pallas kernels for 0%

commit v1 on v0

--- a/solution.py
+++ b/solution.py
@@ -1,9 +1,19 @@
+import functools
 import jax
 import jax.numpy as jnp
 from jax import lax
 from jax.sharding import PartitionSpec as P
 
 precise = lax.Precision.HIGHEST
+
+
+def face_answer(array_here, which_axis):
+    work_now = lax.all_gather(array_here, which_axis)
+    reached = jnp.sum(work_now, axis=0)
+    return reached
+
+
+_advance_sector = functools.partial(face_answer, which_axis=("dp", "ctx"))
 
 
 def carried_in(value, axis, join, neutral):
@@ -133,7 +143,7 @@
         inputs_local, inject_local, read_local, output_grad, log_decay, state_local, incoming
     )
     tokens_all = length * lax.axis_size("dp") * lax.axis_size("ctx")
-    rate_sum = lax.psum(rate_terms, ("dp", "ctx"))
+    rate_sum = _advance_sector(rate_terms)
     return (
         grad_input[None],
         grad_inject[None],

time: 263 us -> 303 us (1.15)
  waiting for transfers between devices: 114 us -> 153 us
    psum x1 -> x0, blocking collectives: 75.2 us -> none  [local(): rate_sum = lax.psum(rate_terms, ('dp', 'ctx'))]
    reduce_scatter x1, waiting for transfers between devices: 21.4 us -> 96.2 us  [local(): lax.psum_scatter(local_weight, 'dp', scatter_dimension=1, tiled=True)]
    unnamed x0 -> x1, blocking collectives: none -> 73.7 us
    reduce_scatter x1, waiting for transfers between devices: 36.1 us -> 0.01 us  [local(): lax.psum_scatter(data_part, 'ctx', scatter_dimension=0, tiled=True)]
  transfers between devices with their start and end apart: 4 -> 4, of which waited for: 4 -> 2; matrix products, arithmetic and copies ran while one was open for 14% -> 12% of each run, Pallas kernels for 0% -> 0%
where the time goes in v1:
time: 303 us; the launch traced here: 300 us
  waiting for transfers between devices  153 us (50%)
  blocking collectives  88.4 us (29%)
  matrix products  33.3 us (11%)
  between operations  14 us (5%)
  other arithmetic  5.98 us (2%)
  local copies, waits for them, and re-layouts  4.99 us (2%)
    reduce_scatter x1, waiting for transfers between devices, local(): lax.psum_scatter(local_weight, 'dp', scatter_dimension=1, tiled=True)  96.2 us
    unnamed x1, blocking collectives  73.7 us
    all_gather x1, waiting for transfers between devices, local(): lax.all_gather(out_weight, 'ctx', axis=1, tiled=True)  56.1 us
    all_gather x1, blocking collectives, carried_in(): pieces = jax.tree.map(lambda part: lax.all_gather(part, axis), value)  14.7 us
    dot_general x1, matrix products, local(): lax.dot_general(outputs, grad_out, (((0,), (0,)), ((), ())), preferred_el...  8.95 us
    dot_general x1, matrix products, local(): lax.dot_general(grad_out, lax.all_gather(out_weight, 'ctx', axis=1, tiled...  6.93 us
  transfers between devices with their start and end apart: 4, of which 2 were waited for; matrix products, arithmetic and copies ran while one was open for 12% of the time, Pallas kernels for 0%

profile of v1, /device:TPU:2, one launch (start us, length us, event | category | flops | bytes accessed | tf_op | source)
XLA Modules:
  0.0 300.1 jit_solution(7296443439108496380)
XLA Ops:
  7.2 0.7 all-gather.6.cloned.1.call-update
  7.9 0.7 neg.4
  8.6 0.8 fusion.61
  9.4 0.6 reduce-window.14
  10.3 0.9 bitcast_convert_fusion.1
  11.5 56.1 %all-gather.6.cloned.1.call-done = bf16[256,8192]{1,0:T(8,128)(2,1)} async-done(((bf16[256,1024]{1,0:T(8,128)(2,1)}), bf16[256,8192]{1,0:T(8,128)(2,1)}) %all-gather.6.cloned.1.call-update) | async-done | bytes 4194320 | tf_op jit(solution)/shard_map/all_gather | solution.py:128
  67.6 6.9 %fusion.26 = bf16[512,256]{0,1:T(8,128)(2,1)S(1)} fusion(bf16[256,8192]{1,0:T(8,128)(2,1)} %all-gather.6.cloned.1.call-done, bf16[1,512,8192]{2,1,0:T(8,128)(2,1)} %param.10), kind=kOutput, calls=%fused_computation.24 | convolution fusion | flops 2147614720 | bytes 12845056 | tf_op jit(solution)/shard_map/dot_general | solution.py:126
  74.6 1.1 fusion.43
  76.8 2.0 fusion.22
  78.7 9.0 %fusion.1 = f32[256,8192]{1,0:T(8,128)} fusion(bf16[512,256]{0,1:T(8,128)(2,1)S(1)} %bitcast.164, bf16[1,512,8192]{2,1,0:T(8,128)(2,1)} %param.10), kind=kOutput, calls=%fused_computation.3 | convolution fusion | flops 2147483648 | bytes 17039360 | tf_op jit(solution)/shard_map/dot_general | solution.py:137
  88.0 14.7 %all-gather.2 = f32[8,1,2]{2,1,0:T(1,128)S(1)} all-gather(f32[1,1,2]{2,1,0:T(1,128)S(1)} %bitcast.175), channel_id=1, replica_groups=mesh['dp'=32,'ctx'=8] {'ctx'}, dimensions={0}, use_global_device_ids=true | all-gather | bytes 72 | tf_op jit(solution)/shard_map/all_gather | solution.py:21
  103.9 3.7 %fusion.45 = f32[512,1,128]{2,1,0:T(1,128)S(1)} fusion(f32[512,2,1]{1,2,0:T(1,128)S(1)} %copy.72, f32[512,2,128]{2,0,1:T(8,128)S(1)} %convolution_bitcast_fusion), kind=kOutput, calls=%fused_computation.47 | convolution fusion | flops 1572864 | bytes 790528 | tf_op jit(solution)/shard_map/th,thn->tn/dot_general | solution.py:91
  107.6 2.2 multiply_reduce_fusion
  109.8 1.3 fusion.29
  111.2 2.4 fusion.11
  113.5 1.3 rev.13
  114.8 0.9 while.14
  117.0 0.6 reduce-window.16
  118.0 1.4 fusion.25
  119.4 96.2 %reduce-scatter.3.cloned.1.call-done = f32[256,256]{1,0:T(8,128)} async-done(((f32[256,8192]{1,0:T(8,128)}), f32[256,256]{1,0:T(8,128)}) %reduce-scatter.3.cloned.1.call-update) | async-done | bytes 262160 | tf_op jit(solution)/shard_map/reduce_scatter | solution.py:140
  215.9 0.8 copy.62
  217.5 73.7 %all-reduce = f32[512]{0:T(512)S(1)} all-reduce(f32[512]{0:T(512)S(1)} %dynamic-update-slice), channel_id=3, replica_groups=mesh['dp'=32,'ctx'=8] {'dp','ctx'}, use_global_device_ids=true, to_apply=%add | all-reduce | flops 512 | bytes 4096
  291.4 1.7 fusion.30
  293.1 0.5 broadcast_multiply_fusion
  (78 shorter events, 6.6 us)
Async XLA Ops:
  7.2 60.4 %all-gather.6.cloned.1.call-start = ((), (), s32[]{:S(2)}) async-start(), calls=%async_computation.2 | async-start | bytes 4718592 | tf_op jit(solution)/shard_map/all_gather | solution.py:128
  7.9 105.6 %all-gather.8.cloned.1.call-start = ((), (), s32[]{:S(2)}) async-start(), calls=%async_computation.5 | async-start | bytes 1179648 | tf_op jit(solution)/shard_map/all_gather | solution.py:21
  11.5 64.2 %copy-start.3 = (bf16[1,512,256]{2,1,0:T(8,128)(2,1)S(1)}, bf16[1,512,256]{2,1,0:T(8,128)(2,1)}, u32[]{:S(2)}) copy-start(bf16[1,512,256]{2,1,0:T(8,128)(2,1)} %param.12) | copy-start | bytes 786436
  11.5 64.5 %copy-start = (bf16[1,512,128]{2,1,0:T(8,128)(2,1)S(1)}, bf16[1,512,128]{2,1,0:T(8,128)(2,1)}, u32[]{:S(2)}) copy-start(bf16[1,512,128]{2,1,0:T(8,128)(2,1)} %param.13) | copy-start | bytes 393220
  11.5 64.5 %copy-start.1 = (bf16[1,512,128]{2,1,0:T(8,128)(2,1)S(1)}, bf16[1,512,128]{2,1,0:T(8,128)(2,1)}, u32[]{:S(2)}) copy-start(bf16[1,512,128]{2,1,0:T(8,128)(2,1)} %param.14) | copy-start | bytes 393220
  74.5 1.8 copy-start.2
  75.7 140.0 %reduce-scatter.3.cloned.1.call-start = ((), (), s32[]{:S(2)}) async-start(), calls=%async_computation.3 | async-start | bytes 8650752 | tf_op jit(solution)/shard_map/reduce_scatter | solution.py:140
  76.0 2.7 copy-start.4
  87.7 205.9 %reduce-scatter.5.cloned.1.call-start = ((), (), s32[]{:S(2)}) async-start(), calls=%async_computation.4 | async-start | bytes 294912 | tf_op jit(solution)/shard_map/reduce_scatter | solution.py:141
  107.6 3.6 %copy-start.5 = (pred[512,512]{1,0:T(8,128)(4,1)S(1)}, pred[512,512]{1,0:T(8,128)(4,1)}, u32[]{:S(2)}) copy-start(pred[512,512]{1,0:T(8,128)(4,1)} %copy-done.4) | copy-start | bytes 786436
  115.9 101.2 %copy-start.6 = (s32[1,512,2]{1,2,0:T(2,128)S(1)}, s32[1,512,2]{1,2,0:T(2,128)}, u32[]{:S(2)}) copy-start(s32[1,512,2]{1,2,0:T(2,128)} %param.15) | copy-start | bytes 12292
Sparse Core Ops, SparseCore 0:
  9.8 57.7 all-gather.5
  75.8 37.3 all-gather.7
  117.1 98.4 reduce-scatter.2
  218.7 36.4 reduce-scatter.4
